TPU v7x, 256 devices: a whole 4x4x8 slice. The times are simulated.
256 devices in a mesh: seq: 32 (over z, y), tp: 8 (over x, core).
Axes of the slice: x: 4, y: 4, z: 8, core: 2. Of those that a mesh axis runs over, the one named last changes fastest.
Arguments:
- tokens: bfloat16 [16384, 4096], P('seq'), may hold values from -80 to 80
- norm_gain: float32 [4096], replicated, may hold values from 0.1 to 1.9
- query_weight: bfloat16 [4096, 4096], P(None, 'tp'), may hold values from -1 to 1
- key_weight: bfloat16 [4096, 1024], P(None, 'tp'), may hold values from -8 to 8
- value_weight: bfloat16 [4096, 1024], P(None, 'tp'), may hold values from -0.09375 to 0.09375
- out_weight: bfloat16 [4096, 4096], P(None, 'tp'), may hold values from -1 to 1
- segments: int32 [16384], replicated, may hold values from 0 to 2, never falling along the last dimension, each value on 1 to 8192 neighbouring positions
Outputs:
- attn_out: bfloat16 [16384, 4096], P('seq', 'tp')
All inputs are finite; a program needn't handle non-finite values.
Results may differ from a plain program's by a relative error of at most 0.013.
The roundings to bfloat16 on the way count: a program that leaves them out, or rounds other values in their place, can miss the bound.
Values may be sent and summed in bfloat16 or wider, within the bound.
A program may use at most 128 MiB of HBM per device.

v0:
```python
import math
import jax
import jax.numpy as jnp
from jax import lax
from jax.sharding import PartitionSpec as P

HEAD_DIM = 128
WINDOW = 4096


def shifted(value, axis, steps):
    count = lax.axis_size(axis)
    leading, last = (max(0, -steps), min(count, count - steps))
    return lax.ppermute(value, axis, [(source, source + steps) for source in range(leading, last)])


def rotate(vectors, positions):
    half_dim = vectors.shape[-1] // 2
    freqs = 10000.0 ** (-(jnp.arange(half_dim, dtype=jnp.float32) * 2.0 / vectors.shape[-1]))
    angles = positions[:, None] * freqs[None, :]
    cosine = jnp.cos(angles)[:, None, :]
    sine_part = jnp.sin(angles)[:, None, :]
    first = vectors[..., :half_dim]
    second = vectors[..., half_dim:]
    return jnp.concatenate(
        [first * cosine - second * sine_part, second * cosine + first * sine_part], axis=-1
    )


def project(normed, weight, positions):
    product = jnp.dot(normed, weight, preferred_element_type=jnp.float32)
    shaped = product.reshape(product.shape[0], -1, HEAD_DIM)
    return rotate(shaped, positions).astype(jnp.bfloat16)


def attend(queries, keys, values, allowed):
    block_rows, query_heads, head_size = queries.shape
    value_heads = keys.shape[1]
    grouped = queries.reshape(block_rows, value_heads, query_heads // value_heads, head_size)
    scores = jnp.einsum(
        "tkgd,skd->kgts", grouped, keys, preferred_element_type=jnp.float32
    ) / math.sqrt(head_size)
    scores = jnp.where(allowed[None, None], scores, jnp.float32(-1e30))
    peak = jnp.max(scores, axis=-1, keepdims=True)
    weights = jnp.exp(scores - peak)
    totals = jnp.sum(weights, axis=-1, keepdims=True)
    probabilities = (weights / totals).astype(jnp.bfloat16)
    attended = jnp.einsum(
        "kgts,skd->tkgd", probabilities, values, preferred_element_type=jnp.float32
    )
    return attended.reshape(block_rows, query_heads * head_size).astype(jnp.bfloat16)


def shards(tokens, norm_gain, query_weight, key_weight, value_weight, out_weight, segments):
    block_rows = tokens.shape[0]
    seq_index = lax.axis_index("seq")
    seq_count = lax.axis_size("seq")
    halo_blocks = min((WINDOW + block_rows - 2) // block_rows, seq_count - 1)
    widened = tokens.astype(jnp.float32)
    scale = lax.rsqrt(jnp.mean(widened * widened, axis=-1, keepdims=True) + 1e-05)
    normed = (widened * scale * norm_gain[None, :]).astype(jnp.bfloat16)
    first_token = seq_index * block_rows
    positions = (first_token + jnp.arange(block_rows, dtype=jnp.int32)).astype(jnp.float32)
    queries = project(normed, query_weight, positions)
    keys = project(normed, key_weight, positions)
    value_heads = keys.shape[1]
    values = jnp.dot(normed, value_weight, preferred_element_type=jnp.float32).astype(jnp.bfloat16)
    key_width = value_heads * HEAD_DIM
    key_value = jnp.concatenate([keys.reshape(block_rows, key_width), values], axis=1)
    front = halo_blocks * block_rows
    known_blocks = key_value
    gathered_count = 0
    while gathered_count < halo_blocks:
        taking = min(gathered_count + 1, halo_blocks - gathered_count)
        outgoing = known_blocks[known_blocks.shape[0] - taking * block_rows :]
        incoming = shifted(outgoing, "seq", gathered_count + 1)
        known_blocks = jnp.concatenate([incoming, known_blocks], axis=0)
        gathered_count = gathered_count + taking
    before = known_blocks[:front]
    window_rows = jnp.concatenate([before, key_value], axis=0)
    span = window_rows.shape[0]
    window_keys = window_rows[:, :key_width].reshape(span, value_heads, HEAD_DIM)
    window_values = window_rows[:, key_width:].reshape(span, value_heads, HEAD_DIM)
    padded_segments = jnp.concatenate([jnp.full((front,), -1, jnp.int32), segments], axis=0)
    start_index = seq_index * block_rows
    key_segments = lax.dynamic_slice_in_dim(padded_segments, start_index, span, 0)
    query_segments = lax.dynamic_slice_in_dim(segments, start_index, block_rows, 0)
    query_pos = start_index + jnp.arange(block_rows, dtype=jnp.int32)
    key_pos = start_index - front + jnp.arange(span, dtype=jnp.int32)
    distance = query_pos[:, None] - key_pos[None, :]
    allowed = (
        (distance >= 0) & (distance < WINDOW) & (key_segments[None, :] == query_segments[:, None])
    )
    attended = attend(queries, window_keys, window_values, allowed)
    projected = jnp.dot(
        lax.all_gather(attended, "tp", axis=1, tiled=True),
        out_weight,
        preferred_element_type=jnp.float32,
    )
    return projected.astype(jnp.bfloat16)


def solution(mesh):
    return jax.shard_map(
        shards,
        mesh=mesh,
        in_specs=(
            P("seq", None),
            P(),
            P(None, "tp"),
            P(None, "tp"),
            P(None, "tp"),
            P(None, "tp"),
            P(),
        ),
        out_specs=P("seq", "tp"),
        check_vma=False,
    )
```

profile of v0, /device:TPU:1, one launch (start us, length us, event | category | flops | bytes accessed | tf_op | source)
XLA Modules:
  0.0 180.7 jit_solution(8147630564713881535)
XLA Ops:
  6.6 0.0 copy-start.2
  6.6 3.2 %fusion.6 = f32[512]{0:T(512)S(1)} fusion(bf16[512,4096]{1,0:T(8,128)(2,1)} %param.7), kind=kLoop, calls=%fused_computation.13 | loop fusion | flops 6290944 | bytes 4196352 | tf_op jit(solution)/shard_map/reduce_sum | solution.py:60
  9.8 0.5 copy-done.2
  10.3 1.6 convolution_convert_fusion.1
  12.0 1.6 convolution_bitcast_fusion
  13.6 0.6 fusion.25
  14.2 0.7 pad_maximum_fusion
  14.9 4.0 %collective-permute-start.1 = (bf16[512,256]{0,1:T(8,128)(2,1)}, bf16[512,256]{0,1:T(8,128)(2,1)S(1)}, u32[]{:S(2)}, u32[]{:S(2)}) collective-permute-start(bf16[512,256]{0,1:T(8,128)(2,1)} %pad_maximum_fusion), channel_id=1, source_target_pairs={{0,8},{8,16},{16,24},{24,32},{32,40},{40,48},{48,56},{56,64},{64,7... | collective-permute-start | bytes 786440 | tf_op jit(solution)/shard_map/ppermute | solution.py:14
  18.9 5.6 %collective-permute-start = (bf16[512,256]{0,1:T(8,128)(2,1)}, bf16[512,256]{0,1:T(8,128)(2,1)}, u32[]{:S(2)}, u32[]{:S(2)}) collective-permute-start(bf16[512,256]{0,1:T(8,128)(2,1)} %pad_maximum_fusion), channel_id=1, source_target_pairs={{0,64},{8,72},{16,80},{24,88},{32,96},{40,104},{48,112},{56,120},{... | collective-permute-start | bytes 786440 | tf_op jit(solution)/shard_map/ppermute | solution.py:14
  24.5 0.1 dynamic_slice.7
  24.6 0.1 pad_dynamic-slice_fusion
  24.7 0.1 maximum_maximum_fusion.1
  24.8 5.3 %collective-permute-start.2 = (bf16[1024,256]{0,1:T(8,128)(2,1)S(1)}, bf16[1024,256]{0,1:T(8,128)(2,1)S(1)}, u32[]{:S(2)}, u32[]{:S(2)}) collective-permute-start(bf16[1024,256]{0,1:T(8,128)(2,1)S(1)} %maximum_maximum_fusion.1), channel_id=1, source_target_pairs={{0,16},{8,24},{16,32},{24,40},{32,48},{40,56},{48,64},{56,72},{64,... | collective-permute-start | bytes 1572872 | tf_op jit(solution)/shard_map/ppermute | solution.py:14
  30.1 3.8 %fusion.5 = pred[512,4608]{0,1:T(8,128)(4,1)S(1)} fusion(s32[512]{0:T(512)S(1)} %dynamic_slice.7, s32[4608]{0:T(1024)S(1)} %get-tuple-element.16, s32[512]{0:T(512)S(1)} %iota_add_fusion.1, s32[4608]{0:T(1024)S(1)} %get-tuple-element.15), kind=kLoop, calls=%fused_computation.12 | loop fusion | flops 14155776 | bytes 2400256 | tf_op jit(solution)/shard_map/and | solution.py:92
  33.8 5.9 %collective-permute-done.2 = bf16[1024,256]{0,1:T(8,128)(2,1)S(1)} collective-permute-done((bf16[1024,256]{0,1:T(8,128)(2,1)S(1)}, bf16[1024,256]{0,1:T(8,128)(2,1)S(1)}, u32[]{:S(2)}, u32[]{:S(2)}) %collective-permute-start.2) | collective-permute-done | bytes 524320 | tf_op jit(solution)/shard_map/ppermute | solution.py:14
  39.7 1.1 maximum_maximum_fusion
  40.9 7.5 %collective-permute-start.3 = (bf16[2048,256]{0,1:T(8,128)(2,1)}, bf16[2048,256]{0,1:T(8,128)(2,1)}, u32[]{:S(2)}, u32[]{:S(2)}) collective-permute-start(bf16[2048,256]{0,1:T(8,128)(2,1)} %maximum_maximum_fusion), channel_id=1, source_target_pairs={{0,32},{8,40},{16,48},{24,56},{32,64},{40,72},{48,80},{56,88},{64,... | collective-permute-start | bytes 3145736 | tf_op jit(solution)/shard_map/ppermute | solution.py:14
  48.4 4.8 %fusion.30 = f32[512,512]{0,1:T(8,128)S(1)} fusion(bf16[4096,512]{1,0:T(8,128)(2,1)} %param.9, bf16[512,4096]{1,0:T(8,128)(2,1)S(1)} %copy-done.3, f32[4096]{0:T(1024)S(1)} %copy-done.16, f32[512]{0:T(512)S(1)} %add_rsqrt_fusion), kind=kOutput, calls=%fused_computation.59 | convolution fusion | flops 2155872256 | bytes 9455616 | tf_op jit(solution)/shard_map/dot_general | solution.py:31
  53.2 1.1 fusion.34
  54.3 1.4 copy.16
  55.6 2.4 %copy.15 = f32[512,4,64]{2,0,1:T(8,128)} copy(f32[512,4,64]{0,2,1:T(8,128)} %get-tuple-element.8) | data formatting | bytes 1048576
  58.0 1.0 multiply_cosine_fusion
  59.0 1.5 subtract_convert_fusion
  60.6 1.0 constant_dynamic-update-slice_fusion.4
  61.5 5.6 %collective-permute-done.3 = bf16[2048,256]{0,1:T(8,128)(2,1)} collective-permute-done((bf16[2048,256]{0,1:T(8,128)(2,1)}, bf16[2048,256]{0,1:T(8,128)(2,1)}, u32[]{:S(2)}, u32[]{:S(2)}) %collective-permute-start.3) | collective-permute-done | bytes 1048608 | tf_op jit(solution)/shard_map/ppermute | solution.py:14
  67.1 1.3 constant_dynamic-update-slice_fusion.3
  68.6 15.3 %fusion.1 = (f32[4,512]{1,0:T(4,128)S(1)}, f32[4608,512,4]{1,0,2:T(8,128)}) fusion(pred[512,4608]{0,1:T(8,128)(4,1)S(1)} %fusion.5, bf16[512,4,64]{2,0,1:T(8,128)(2,1)S(1)} %get-tuple-element.6, bf16[512,4,64]{2,0,1:T(8,128)(2,1)S(1)} %get-tuple-element.5, bf16[4608,256]{0,1:T(8,128)(2,1)S(1)} %constant_dynamic-update-slice_fusion), kind=kOutput, calls=%fused_computation.4 | convolution fusion | flops 2445277184 | bytes 42344448 | tf_op jit(solution)/shard_map/tkgd,skd->kgts/dot_general | solution.py:40
  83.9 16.0 %fusion = f32[4,512]{1,0:T(4,128)S(1)} fusion(f32[4608,512,4]{1,0,2:T(8,128)} %get-tuple-element.14, f32[4,512]{1,0:T(4,128)S(1)} %get-tuple-element.13, pred[512,4608]{0,1:T(8,128)(4,1)S(1)} %fusion.5), kind=kLoop, calls=%fused_computation.3 | loop fusion | flops 37746688 | bytes 40124416 | tf_op jit(solution)/shard_map/reduce_sum | solution.py:46
  99.9 18.3 %fusion.9 = bf16[128,4,512]{2,0,1:T(8,128)(2,1)} fusion(f32[4,512]{1,0:T(4,128)S(1)} %fusion, f32[4,512]{1,0:T(4,128)S(1)} %get-tuple-element.13, f32[4608,512,4]{1,0,2:T(8,128)} %get-tuple-element.14, pred[512,4608]{0,1:T(8,128)(4,1)S(1)} %fusion.5, bf16[4608,256]{0,1:T(8,128)(2,1)} %copy-done.13), kind=kOutput, calls=%fused_computation.17 | convolution fusion | flops 2463367168 | bytes 41828352 | tf_op jit(solution)/shard_map/kgts,skd->tkgd/dot_general | solution.py:48
  118.2 0.0 all-gather.2.cloned.1.call-update
  118.3 48.9 %all-gather.2.cloned.1.call-done = bf16[512,4096]{0,1:T(8,128)(2,1)} async-done(((bf16[512,512]{0,1:T(8,128)(2,1)}), bf16[512,4096]{0,1:T(8,128)(2,1)}) %all-gather.2.cloned.1.call-update) | async-done | bytes 4194320 | tf_op jit(solution)/shard_map/all_gather | solution.py:96
  167.2 6.6 %convolution_convert_fusion = bf16[512,512]{1,0:T(8,128)(2,1)} fusion(bf16[512,4096]{0,1:T(8,128)(2,1)} %all-gather.2.cloned.1.call-done, bf16[4096,512]{1,0:T(8,128)(2,1)} %param.12), kind=kOutput, calls=%fused_computation.16 | convolution fusion | flops 2147745792 | bytes 8912896 | tf_op jit(solution)/shard_map/dot_general | solution.py:95
  (42 shorter events, 0.2 us)
Async XLA Ops:
  6.5 3.3 %copy-start = (bf16[4096,128]{1,0:T(8,128)(2,1)S(1)}, bf16[4096,128]{1,0:T(8,128)(2,1)}, u32[]{:S(2)}) copy-start(bf16[4096,128]{1,0:T(8,128)(2,1)} %param.11) | copy-start | bytes 3145732
  6.5 3.3 %copy-start.15 = (f32[4096]{0:T(1024)S(1)}, f32[4096]{0:T(1024)}, u32[]{:S(2)}) copy-start(f32[4096]{0:T(1024)} %param.8) | copy-start | bytes 49156
  6.5 160.7 %all-gather.2.cloned.1.call-start = ((), (), s32[]{:S(2)}) async-start(), calls=%async_computation | async-start | bytes 4718592 | tf_op jit(solution)/shard_map/all_gather | solution.py:96
  6.6 3.8 %copy-start.2 = (bf16[512,4096]{1,0:T(8,128)(2,1)S(1)}, bf16[512,4096]{1,0:T(8,128)(2,1)}, u32[]{:S(2)}) copy-start(bf16[512,4096]{1,0:T(8,128)(2,1)} %param.7) | copy-start | bytes 12582916
  10.3 1.6 copy-start.14
  12.0 12.6 %copy-start.12 = (s32[16384]{0:T(1024)S(1)}, s32[16384]{0:T(1024)}, u32[]{:S(2)}) copy-start(s32[16384]{0:T(1024)} %param.13) | copy-start | bytes 196612
  13.6 34.8 %copy-start.16 = (f32[4096]{0:T(1024)S(1)}, f32[4096]{0:T(1024)}, u32[]{:S(2)}) copy-start(f32[4096]{0:T(1024)} %param.8) | copy-start | bytes 49156
  14.2 39.0 %copy-start.8 = (bf16[512,64]{0,1:T(8,128)(2,1)}, bf16[512,64]{0,1:T(8,128)(2,1)S(1)}, u32[]{:S(2)}) copy-start(bf16[512,64]{0,1:T(8,128)(2,1)S(1)} %get-tuple-element.9) | copy-start | bytes 196612
  14.2 39.0 %copy-start.10 = (bf16[512,64]{0,1:T(8,128)(2,1)}, bf16[512,64]{0,1:T(8,128)(2,1)S(1)}, u32[]{:S(2)}) copy-start(bf16[512,64]{0,1:T(8,128)(2,1)S(1)} %get-tuple-element.10) | copy-start | bytes 196612
  14.9 9.8 %collective-permute-start.1 = (bf16[512,256]{0,1:T(8,128)(2,1)}, bf16[512,256]{0,1:T(8,128)(2,1)S(1)}, u32[]{:S(2)}, u32[]{:S(2)}) collective-permute-start(bf16[512,256]{0,1:T(8,128)(2,1)} %pad_maximum_fusion), channel_id=1, source_target_pairs={{0,8},{8,16},{16,24},{24,32},{32,40},{40,48},{48,56},{56,64},{64,7... | collective-permute-start | bytes 786440 | tf_op jit(solution)/shard_map/ppermute | solution.py:14
  18.9 41.6 %collective-permute-start = (bf16[512,256]{0,1:T(8,128)(2,1)}, bf16[512,256]{0,1:T(8,128)(2,1)}, u32[]{:S(2)}, u32[]{:S(2)}) collective-permute-start(bf16[512,256]{0,1:T(8,128)(2,1)} %pad_maximum_fusion), channel_id=1, source_target_pairs={{0,64},{8,72},{16,80},{24,88},{32,96},{40,104},{48,112},{56,120},{... | collective-permute-start | bytes 786440 | tf_op jit(solution)/shard_map/ppermute | solution.py:14
  24.5 23.9 %copy-start.3 = (bf16[512,4096]{1,0:T(8,128)(2,1)S(1)}, bf16[512,4096]{1,0:T(8,128)(2,1)}, u32[]{:S(2)}) copy-start(bf16[512,4096]{1,0:T(8,128)(2,1)} %param.7) | copy-start | bytes 12582916
  24.7 28.5 %copy-start.4 = (bf16[512,256]{0,1:T(8,128)(2,1)}, bf16[512,256]{0,1:T(8,128)(2,1)S(1)}, u32[]{:S(2)}) copy-start(bf16[512,256]{0,1:T(8,128)(2,1)S(1)} %collective-permute-done.1) | copy-start | bytes 786436
  24.8 15.0 %collective-permute-start.2 = (bf16[1024,256]{0,1:T(8,128)(2,1)S(1)}, bf16[1024,256]{0,1:T(8,128)(2,1)S(1)}, u32[]{:S(2)}, u32[]{:S(2)}) collective-permute-start(bf16[1024,256]{0,1:T(8,128)(2,1)S(1)} %maximum_maximum_fusion.1), channel_id=1, source_target_pairs={{0,16},{8,24},{16,32},{24,40},{32,48},{40,56},{48,64},{56,72},{64,... | collective-permute-start | bytes 1572872 | tf_op jit(solution)/shard_map/ppermute | solution.py:14
  39.7 13.5 %copy-start.6 = (bf16[1024,256]{0,1:T(8,128)(2,1)}, bf16[1024,256]{0,1:T(8,128)(2,1)S(1)}, u32[]{:S(2)}) copy-start(bf16[1024,256]{0,1:T(8,128)(2,1)S(1)} %collective-permute-done.2) | copy-start | bytes 1572868
  40.9 26.3 %collective-permute-start.3 = (bf16[2048,256]{0,1:T(8,128)(2,1)}, bf16[2048,256]{0,1:T(8,128)(2,1)}, u32[]{:S(2)}, u32[]{:S(2)}) collective-permute-start(bf16[2048,256]{0,1:T(8,128)(2,1)} %maximum_maximum_fusion), channel_id=1, source_target_pairs={{0,32},{8,40},{16,48},{24,56},{32,64},{40,72},{48,80},{56,88},{64,... | collective-permute-start | bytes 3145736 | tf_op jit(solution)/shard_map/ppermute | solution.py:14
  58.0 10.4 %copy-start.7 = (bf16[1024,256]{0,1:T(8,128)(2,1)S(1)}, bf16[1024,256]{0,1:T(8,128)(2,1)}, u32[]{:S(2)}) copy-start(bf16[1024,256]{0,1:T(8,128)(2,1)} %copy-done.6) | copy-start | bytes 1572868
  58.0 10.5 %copy-start.5 = (bf16[512,256]{0,1:T(8,128)(2,1)S(1)}, bf16[512,256]{0,1:T(8,128)(2,1)}, u32[]{:S(2)}) copy-start(bf16[512,256]{0,1:T(8,128)(2,1)} %copy-done.4) | copy-start | bytes 786436
  58.0 10.5 %copy-start.9 = (bf16[512,64]{0,1:T(8,128)(2,1)S(1)}, bf16[512,64]{0,1:T(8,128)(2,1)}, u32[]{:S(2)}) copy-start(bf16[512,64]{0,1:T(8,128)(2,1)} %copy-done.8) | copy-start | bytes 196612
  58.0 10.5 %copy-start.11 = (bf16[512,64]{0,1:T(8,128)(2,1)S(1)}, bf16[512,64]{0,1:T(8,128)(2,1)}, u32[]{:S(2)}) copy-start(bf16[512,64]{0,1:T(8,128)(2,1)} %copy-done.10) | copy-start | bytes 196612
  68.6 15.3 %copy-start.13 = (bf16[4608,256]{0,1:T(8,128)(2,1)}, bf16[4608,256]{0,1:T(8,128)(2,1)S(1)}, u32[]{:S(2)}) copy-start(bf16[4608,256]{0,1:T(8,128)(2,1)S(1)} %constant_dynamic-update-slice_fusion) | copy-start | bytes 7077892
  118.3 55.5 %copy-start.1 = (bf16[4096,128]{1,0:T(8,128)(2,1)S(1)}, bf16[4096,128]{1,0:T(8,128)(2,1)}, u32[]{:S(2)}) copy-start(bf16[4096,128]{1,0:T(8,128)(2,1)} %param.11) | copy-start | bytes 3145732
Sparse Core Ops, SparseCore 0:
  118.4 48.7 all-gather.1
where the time goes:
time: 181 us
  waiting for transfers between devices  60.5 us (33%)
  matrix products  48.2 us (27%)
  other arithmetic  28.1 us (16%)
  starting transfers between devices  22.4 us (12%)
  between operations  13.7 us (8%)
  local copies, waits for them, and re-layouts  7.74 us (4%)
    all_gather x1, waiting for transfers between devices, shards(): lax.all_gather(attended, 'tp', axis=1, tiled=True)  48.9 us
    ppermute x4, starting transfers between devices, shifted(): lax.ppermute(value, axis, [(source, source + steps) for source in range(l...  22.4 us
    dot_general x1, matrix products, attend(): jnp.einsum('kgts,skd->tkgd', probabilities, values, preferred_element_typ...  18.3 us
    reduce_sum x1, other arithmetic, attend(): totals = jnp.sum(weights, axis=-1, keepdims=True)  16 us
    dot_general x1, matrix products, attend(): jnp.einsum('tkgd,skd->kgts', grouped, keys, preferred_element_type=jnp.fl...  15.3 us
    ppermute x4, waiting for transfers between devices, shifted(): lax.ppermute(value, axis, [(source, source + steps) for source in range(l...  11.6 us
    unnamed x40, local copies, waits for them, and re-layouts  6.61 us
    dot_general x1, matrix products, shards(): jnp.dot(lax.all_gather(attended, 'tp', axis=1, tiled=True), out_weight, p...  6.61 us
  transfers between devices with their start and end apart: 5, of which 3 were waited for; matrix products, arithmetic and copies ran while one was open for 10% of the time, Pallas kernels for 0%

commit v1 on v0

--- a/solution.py
+++ b/solution.py
@@ -1,3 +1,4 @@
+import functools
 import math
 import jax
 import jax.numpy as jnp
@@ -6,6 +7,26 @@
 
 HEAD_DIM = 128
 WINDOW = 4096
+
+
+def reach_the_tokens(xs, shard_axis):
+    k_all = lax.psum(1, axis_name=shard_axis)
+    seen = [(h, (h + 1) % k_all) for h in range(k_all)]
+    bank = [(h, (h - 1) % k_all) for h in range(k_all)]
+    near, then = ([xs], [xs])
+    for _ in range(k_all // 2):
+        near.append(lax.ppermute(near[-1], perm=seen, axis_name=shard_axis))
+    k = 0
+    while k < (k_all - 1) // 2:
+        part_now = lax.ppermute(then[-1], axis_name=shard_axis, perm=bank)
+        then.append(part_now)
+        k += 1
+    frame_out = jnp.concatenate([*near[::-1], *then[1:]], 1)
+    val2 = jnp.roll(frame_out, (lax.axis_index(shard_axis) - k_all // 2) * xs.shape[1], 1)
+    return val2
+
+
+change_the_shards = functools.partial(reach_the_tokens, shard_axis="tp")
 
 
 def shifted(value, axis, steps):
@@ -92,11 +113,7 @@
         (distance >= 0) & (distance < WINDOW) & (key_segments[None, :] == query_segments[:, None])
     )
     attended = attend(queries, window_keys, window_values, allowed)
-    projected = jnp.dot(
-        lax.all_gather(attended, "tp", axis=1, tiled=True),
-        out_weight,
-        preferred_element_type=jnp.float32,
-    )
+    projected = jnp.dot(change_the_shards(attended), out_weight, preferred_element_type=jnp.float32)
     return projected.astype(jnp.bfloat16)
 
 

time: 181 us -> 172 us (0.950)
  the two profiles are of different devices: /device:TPU:1 before, /device:TPU:136 now
where the time goes in v1:
time: 172 us
  waiting for transfers between devices  61.9 us (36%)
  matrix products  47.4 us (28%)
  other arithmetic  28.2 us (16%)
  starting transfers between devices  21.9 us (13%)
  local copies, waits for them, and re-layouts  11.9 us (7%)
    ppermute x4, waiting for transfers between devices, shifted(): lax.ppermute(value, axis, [(source, source + steps) for source in range(l...  31.4 us
    ppermute x4, waiting for transfers between devices, reach_the_tokens(): near.append(lax.ppermute(near[-1], perm=seen, axis_name=shard_axis))  30.5 us
    dot_general x1, matrix products, attend(): jnp.einsum('kgts,skd->tkgd', probabilities, values, preferred_element_typ...  17.6 us
    reduce_sum x1, other arithmetic, attend(): totals = jnp.sum(weights, axis=-1, keepdims=True)  16 us
    dot_general x1, matrix products, attend(): jnp.einsum('tkgd,skd->kgts', grouped, keys, preferred_element_type=jnp.fl...  15.3 us
    ppermute x4, starting transfers between devices, shifted(): lax.ppermute(value, axis, [(source, source + steps) for source in range(l...  13 us
    unnamed x51, local copies, waits for them, and re-layouts  10.7 us
    ppermute x3, starting transfers between devices, reach_the_tokens(): part_now = lax.ppermute(then[-1], axis_name=shard_axis, perm=bank)  8.86 us
  transfers between devices with their start and end apart: 11, of which 7 were waited for; matrix products, arithmetic and copies ran while one was open for 12% of the time, Pallas kernels for 0%

profile of v1, /device:TPU:136, one launch (start us, length us, event | category | flops | bytes accessed | tf_op | source)
XLA Modules:
  0.0 171.7 jit_solution(16664720759393424545)
XLA Ops:
  0.1 3.2 %fusion.6 = f32[512]{0:T(512)S(1)} fusion(bf16[512,4096]{1,0:T(8,128)(2,1)} %param.7), kind=kLoop, calls=%fused_computation.13 | loop fusion | flops 6290944 | bytes 4196352 | tf_op jit(solution)/shard_map/reduce_sum | solution.py:81
  3.3 3.8 %convolution_convert_fusion = bf16[512,128]{0,1:T(8,128)(2,1)S(1)} fusion(bf16[4096,128]{1,0:T(8,128)(2,1)S(1)} %copy-done, bf16[512,4096]{1,0:T(8,128)(2,1)} %param.7, f32[4096]{0:T(1024)} %param.8, f32[512]{0:T(512)S(1)} %add_rsqrt_fusion), kind=kOutput, calls=%fused_computation.24 | convolution fusion | flops 545325056 | bytes 5392384 | tf_op jit(solution)/shard_map/dot_general | solution.py:88
  7.2 1.6 convolution_bitcast_fusion
  10.1 3.5 %collective-permute-start.1 = (bf16[512,256]{0,1:T(8,128)(2,1)}, bf16[512,256]{0,1:T(8,128)(2,1)S(1)}, u32[]{:S(2)}, u32[]{:S(2)}) collective-permute-start(bf16[512,256]{0,1:T(8,128)(2,1)} %pad_maximum_fusion), channel_id=1, source_target_pairs={{0,8},{8,16},{16,24},{24,32},{32,40},{40,48},{48,56},{56,64},{64,7... | collective-permute-start | bytes 786440 | tf_op jit(solution)/shard_map/ppermute | solution.py:35
  13.6 3.4 %collective-permute-start = (bf16[512,256]{0,1:T(8,128)(2,1)}, bf16[512,256]{0,1:T(8,128)(2,1)}, u32[]{:S(2)}, u32[]{:S(2)}) collective-permute-start(bf16[512,256]{0,1:T(8,128)(2,1)} %pad_maximum_fusion), channel_id=1, source_target_pairs={{0,64},{8,72},{16,80},{24,88},{32,96},{40,104},{48,112},{56,120},{... | collective-permute-start | bytes 786440 | tf_op jit(solution)/shard_map/ppermute | solution.py:35
  17.2 3.1 %collective-permute-done.1 = bf16[512,256]{0,1:T(8,128)(2,1)S(1)} collective-permute-done((bf16[512,256]{0,1:T(8,128)(2,1)}, bf16[512,256]{0,1:T(8,128)(2,1)S(1)}, u32[]{:S(2)}, u32[]{:S(2)}) %collective-permute-start.1) | collective-permute-done | bytes 262176 | tf_op jit(solution)/shard_map/ppermute | solution.py:35
  20.3 4.2 %collective-permute-start.2 = (bf16[1024,256]{0,1:T(8,128)(2,1)S(1)}, bf16[1024,256]{0,1:T(8,128)(2,1)S(1)}, u32[]{:S(2)}, u32[]{:S(2)}) collective-permute-start(bf16[1024,256]{0,1:T(8,128)(2,1)S(1)} %maximum_maximum_fusion.1), channel_id=1, source_target_pairs={{0,16},{8,24},{16,32},{24,40},{32,48},{40,56},{48,64},{56,72},{64,... | collective-permute-start | bytes 1572872 | tf_op jit(solution)/shard_map/ppermute | solution.py:35
  24.5 3.8 %fusion.5 = pred[512,4608]{0,1:T(8,128)(4,1)S(1)} fusion(s32[512]{0:T(512)S(1)} %dynamic_slice.11, s32[4608]{0:T(1024)S(1)} %get-tuple-element.16, s32[512]{0:T(512)S(1)} %iota_add_fusion.1, s32[4608]{0:T(1024)S(1)} %get-tuple-element.15), kind=kLoop, calls=%fused_computation.12 | loop fusion | flops 14155776 | bytes 2400256 | tf_op jit(solution)/shard_map/and | solution.py:113
  28.3 17.1 %collective-permute-done.2 = bf16[1024,256]{0,1:T(8,128)(2,1)S(1)} collective-permute-done((bf16[1024,256]{0,1:T(8,128)(2,1)S(1)}, bf16[1024,256]{0,1:T(8,128)(2,1)S(1)}, u32[]{:S(2)}, u32[]{:S(2)}) %collective-permute-start.2) | collective-permute-done | bytes 524320 | tf_op jit(solution)/shard_map/ppermute | solution.py:35
  45.4 1.1 maximum_maximum_fusion
  46.5 1.9 %collective-permute-start.3 = (bf16[2048,256]{0,1:T(8,128)(2,1)}, bf16[2048,256]{0,1:T(8,128)(2,1)}, u32[]{:S(2)}, u32[]{:S(2)}) collective-permute-start(bf16[2048,256]{0,1:T(8,128)(2,1)} %maximum_maximum_fusion), channel_id=1, source_target_pairs={{0,32},{8,40},{16,48},{24,56},{32,64},{40,72},{48,80},{56,88},{64,... | collective-permute-start | bytes 3145736 | tf_op jit(solution)/shard_map/ppermute | solution.py:35
  48.5 5.9 %fusion.36 = f32[512,512]{0,1:T(8,128)S(1)} fusion(bf16[4096,512]{1,0:T(8,128)(2,1)} %param.9, bf16[512,4096]{1,0:T(8,128)(2,1)} %param.7, f32[4096]{0:T(1024)S(1)} %copy-done.14, f32[512]{0:T(512)S(1)} %add_rsqrt_fusion), kind=kOutput, calls=%fused_computation.78 | convolution fusion | flops 2155872256 | bytes 9455616 | tf_op jit(solution)/shard_map/dot_general | solution.py:52
  54.4 1.1 fusion.40
  55.5 1.4 copy.16
  56.9 2.4 %copy.15 = f32[512,4,64]{2,0,1:T(8,128)} copy(f32[512,4,64]{0,2,1:T(8,128)} %get-tuple-element.8) | data formatting | bytes 1048576
  60.2 1.5 subtract_convert_fusion
  62.8 11.2 %collective-permute-done.3 = bf16[2048,256]{0,1:T(8,128)(2,1)} collective-permute-done((bf16[2048,256]{0,1:T(8,128)(2,1)}, bf16[2048,256]{0,1:T(8,128)(2,1)}, u32[]{:S(2)}, u32[]{:S(2)}) %collective-permute-start.3) | collective-permute-done | bytes 1048608 | tf_op jit(solution)/shard_map/ppermute | solution.py:35
  74.0 1.3 constant_dynamic-update-slice_fusion.3
  75.3 1.1 constant_dynamic-update-slice_fusion.2
  77.4 15.3 %fusion.1 = (f32[4,512]{1,0:T(4,128)S(1)}, f32[4608,512,4]{1,0,2:T(8,128)}) fusion(pred[512,4608]{0,1:T(8,128)(4,1)S(1)} %fusion.5, bf16[512,4,64]{2,0,1:T(8,128)(2,1)S(1)} %get-tuple-element.6, bf16[512,4,64]{2,0,1:T(8,128)(2,1)S(1)} %get-tuple-element.5, bf16[4608,256]{0,1:T(8,128)(2,1)S(1)} %constant_dynamic-update-slice_fusion), kind=kOutput, calls=%fused_computation.4 | convolution fusion | flops 2445277184 | bytes 42344448 | tf_op jit(solution)/shard_map/tkgd,skd->kgts/dot_general | solution.py:61
  92.7 16.0 %fusion = f32[4,512]{1,0:T(4,128)S(1)} fusion(f32[4608,512,4]{1,0,2:T(8,128)} %get-tuple-element.14, f32[4,512]{1,0:T(4,128)S(1)} %get-tuple-element.13, pred[512,4608]{0,1:T(8,128)(4,1)S(1)} %fusion.5), kind=kLoop, calls=%fused_computation.3 | loop fusion | flops 37746688 | bytes 40124416 | tf_op jit(solution)/shard_map/reduce_sum | solution.py:67
  108.7 17.6 %fusion.14 = bf16[128,4,512]{2,0,1:T(8,128)(2,1)S(1)} fusion(f32[4,512]{1,0:T(4,128)S(1)} %fusion, f32[4,512]{1,0:T(4,128)S(1)} %get-tuple-element.13, f32[4608,512,4]{1,0,2:T(8,128)} %get-tuple-element.14, pred[512,4608]{0,1:T(8,128)(4,1)S(1)} %fusion.5, bf16[4608,256]{0,1:T(8,128)(2,1)} %copy-done.10), kind=kOutput, calls=%fused_computation.19 | convolution fusion | flops 2463367168 | bytes 41828352 | tf_op jit(solution)/shard_map/kgts,skd->tkgd/dot_general | solution.py:69
  126.4 9.8 %collective-permute-done.4 = bf16[512,512]{0,1:T(8,128)(2,1)S(1)} collective-permute-done((bf16[512,512]{0,1:T(8,128)(2,1)S(1)}, bf16[512,512]{0,1:T(8,128)(2,1)S(1)}, u32[]{:S(2)}, u32[]{:S(2)}) %collective-permute-start.4) | collective-permute-done | bytes 524320 | tf_op jit(solution)/shard_map/ppermute | solution.py:18
  136.2 3.0 %collective-permute-start.8 = (bf16[512,512]{0,1:T(8,128)(2,1)S(1)}, bf16[512,512]{0,1:T(8,128)(2,1)S(1)}, u32[]{:S(2)}, u32[]{:S(2)}) collective-permute-start(bf16[512,512]{0,1:T(8,128)(2,1)S(1)} %bitcast.45), channel_id=1, source_target_pairs={{0,7},{1,0},{2,1},{3,2},{4,3},{5,4},{6,5},{7,6},{8,15},{9,8},{10,9... | collective-permute-start | bytes 1572872 | tf_op jit(solution)/shard_map/ppermute | solution.py:21
  139.2 6.9 %collective-permute-done.5 = bf16[512,512]{0,1:T(8,128)(2,1)S(1)} collective-permute-done((bf16[512,512]{0,1:T(8,128)(2,1)S(1)}, bf16[512,512]{0,1:T(8,128)(2,1)S(1)}, u32[]{:S(2)}, u32[]{:S(2)}) %collective-permute-start.5) | collective-permute-done | bytes 524320 | tf_op jit(solution)/shard_map/ppermute | solution.py:18
  146.0 3.0 %collective-permute-start.9 = (bf16[512,512]{0,1:T(8,128)(2,1)S(1)}, bf16[512,512]{0,1:T(8,128)(2,1)S(1)}, u32[]{:S(2)}, u32[]{:S(2)}) collective-permute-start(bf16[512,512]{0,1:T(8,128)(2,1)S(1)} %collective-permute-done.8), channel_id=1, source_target_pairs={{0,7},{1,0},{2,1},{3,2},{4,3},{5,4},{6,5},{7,6},{8,15},{9,8},{10,9... | collective-permute-start | bytes 1572872 | tf_op jit(solution)/shard_map/ppermute | solution.py:21
  149.0 6.9 %collective-permute-done.6 = bf16[512,512]{0,1:T(8,128)(2,1)S(1)} collective-permute-done((bf16[512,512]{0,1:T(8,128)(2,1)S(1)}, bf16[512,512]{0,1:T(8,128)(2,1)S(1)}, u32[]{:S(2)}, u32[]{:S(2)}) %collective-permute-start.6) | collective-permute-done | bytes 524320 | tf_op jit(solution)/shard_map/ppermute | solution.py:18
  155.8 3.0 %collective-permute-start.10 = (bf16[512,512]{0,1:T(8,128)(2,1)S(1)}, bf16[512,512]{0,1:T(8,128)(2,1)S(1)}, u32[]{:S(2)}, u32[]{:S(2)}) collective-permute-start(bf16[512,512]{0,1:T(8,128)(2,1)S(1)} %collective-permute-done.9), channel_id=1, source_target_pairs={{0,7},{1,0},{2,1},{3,2},{4,3},{5,4},{6,5},{7,6},{8,15},{9,8},{10,9... | collective-permute-start | bytes 1572872 | tf_op jit(solution)/shard_map/ppermute | solution.py:21
  158.8 7.0 %collective-permute-done.7 = bf16[512,512]{0,1:T(8,128)(2,1)} collective-permute-done((bf16[512,512]{0,1:T(8,128)(2,1)S(1)}, bf16[512,512]{0,1:T(8,128)(2,1)}, u32[]{:S(2)}, u32[]{:S(2)}) %collective-permute-start.7) | collective-permute-done | bytes 524320 | tf_op jit(solution)/shard_map/ppermute | solution.py:18
  165.8 1.1 constant_dynamic-update-slice_fusion.20
  167.2 1.1 constant_dynamic-update-slice_fusion.12
  168.6 3.2 %fusion.11 = bf16[512,512]{1,0:T(8,128)(2,1)} fusion(bf16[4096,512]{1,0:T(8,128)(2,1)S(1)} %copy-done.11, bf16[512,8192]{0,1:T(8,128)(2,1)S(1)} %constant_dynamic-update-slice_fusion.5, s32[]{:T(128)S(6)} %select_n.27), kind=kOutput, calls=%fused_computation.18 | convolution fusion | flops 2147745792 | bytes 8912900 | tf_op jit(solution)/shard_map/dot_general | solution.py:116
  (65 shorter events, 5.1 us)
Async XLA Ops:
  0.0 3.3 %copy-start = (bf16[4096,128]{1,0:T(8,128)(2,1)S(1)}, bf16[4096,128]{1,0:T(8,128)(2,1)}, u32[]{:S(2)}) copy-start(bf16[4096,128]{1,0:T(8,128)(2,1)} %param.11) | copy-start | bytes 3145732
  0.0 7.1 %copy-start.13 = (f32[4096]{0:T(1024)S(1)}, f32[4096]{0:T(1024)}, u32[]{:S(2)}) copy-start(f32[4096]{0:T(1024)} %param.8) | copy-start | bytes 49156
  0.0 7.1 %copy-start.12 = (bf16[4096,128]{1,0:T(8,128)(2,1)S(1)}, bf16[4096,128]{1,0:T(8,128)(2,1)}, u32[]{:S(2)}) copy-start(bf16[4096,128]{1,0:T(8,128)(2,1)} %param.10) | copy-start | bytes 3145732
  0.0 7.1 %copy-start.2 = (bf16[512,4096]{1,0:T(8,128)(2,1)S(1)}, bf16[512,4096]{1,0:T(8,128)(2,1)}, u32[]{:S(2)}) copy-start(bf16[512,4096]{1,0:T(8,128)(2,1)} %param.7) | copy-start | bytes 12582916
  7.1 9.9 %copy-start.9 = (s32[16384]{0:T(1024)S(1)}, s32[16384]{0:T(1024)}, u32[]{:S(2)}) copy-start(s32[16384]{0:T(1024)} %param.13) | copy-start | bytes 196612
  7.2 41.3 %copy-start.14 = (f32[4096]{0:T(1024)S(1)}, f32[4096]{0:T(1024)}, u32[]{:S(2)}) copy-start(f32[4096]{0:T(1024)} %param.8) | copy-start | bytes 49156
  9.3 45.1 %copy-start.5 = (bf16[512,64]{0,1:T(8,128)(2,1)}, bf16[512,64]{0,1:T(8,128)(2,1)S(1)}, u32[]{:S(2)}) copy-start(bf16[512,64]{0,1:T(8,128)(2,1)S(1)} %get-tuple-element.9) | copy-start | bytes 196612
  9.4 45.1 %copy-start.7 = (bf16[512,64]{0,1:T(8,128)(2,1)}, bf16[512,64]{0,1:T(8,128)(2,1)S(1)}, u32[]{:S(2)}) copy-start(bf16[512,64]{0,1:T(8,128)(2,1)S(1)} %get-tuple-element.10) | copy-start | bytes 196612
  10.1 10.1 %collective-permute-start.1 = (bf16[512,256]{0,1:T(8,128)(2,1)}, bf16[512,256]{0,1:T(8,128)(2,1)S(1)}, u32[]{:S(2)}, u32[]{:S(2)}) collective-permute-start(bf16[512,256]{0,1:T(8,128)(2,1)} %pad_maximum_fusion), channel_id=1, source_target_pairs={{0,8},{8,16},{16,24},{24,32},{32,40},{40,48},{48,56},{56,64},{64,7... | collective-permute-start | bytes 786440 | tf_op jit(solution)/shard_map/ppermute | solution.py:35
  13.6 48.2 %collective-permute-start = (bf16[512,256]{0,1:T(8,128)(2,1)}, bf16[512,256]{0,1:T(8,128)(2,1)}, u32[]{:S(2)}, u32[]{:S(2)}) collective-permute-start(bf16[512,256]{0,1:T(8,128)(2,1)} %pad_maximum_fusion), channel_id=1, source_target_pairs={{0,64},{8,72},{16,80},{24,88},{32,96},{40,104},{48,112},{56,120},{... | collective-permute-start | bytes 786440 | tf_op jit(solution)/shard_map/ppermute | solution.py:35
  20.3 34.2 %copy-start.3 = (bf16[512,256]{0,1:T(8,128)(2,1)}, bf16[512,256]{0,1:T(8,128)(2,1)S(1)}, u32[]{:S(2)}) copy-start(bf16[512,256]{0,1:T(8,128)(2,1)S(1)} %collective-permute-done.1) | copy-start | bytes 786436
  20.3 25.1 %collective-permute-start.2 = (bf16[1024,256]{0,1:T(8,128)(2,1)S(1)}, bf16[1024,256]{0,1:T(8,128)(2,1)S(1)}, u32[]{:S(2)}, u32[]{:S(2)}) collective-permute-start(bf16[1024,256]{0,1:T(8,128)(2,1)S(1)} %maximum_maximum_fusion.1), channel_id=1, source_target_pairs={{0,16},{8,24},{16,32},{24,40},{32,48},{40,56},{48,64},{56,72},{64,... | collective-permute-start | bytes 1572872 | tf_op jit(solution)/shard_map/ppermute | solution.py:35
  45.4 9.0 %copy-start.4 = (bf16[1024,256]{0,1:T(8,128)(2,1)}, bf16[1024,256]{0,1:T(8,128)(2,1)S(1)}, u32[]{:S(2)}) copy-start(bf16[1024,256]{0,1:T(8,128)(2,1)S(1)} %collective-permute-done.2) | copy-start | bytes 1572868
  46.5 27.5 %collective-permute-start.3 = (bf16[2048,256]{0,1:T(8,128)(2,1)}, bf16[2048,256]{0,1:T(8,128)(2,1)}, u32[]{:S(2)}, u32[]{:S(2)}) collective-permute-start(bf16[2048,256]{0,1:T(8,128)(2,1)} %maximum_maximum_fusion), channel_id=1, source_target_pairs={{0,32},{8,40},{16,48},{24,56},{32,64},{40,72},{48,80},{56,88},{64,... | collective-permute-start | bytes 3145736 | tf_op jit(solution)/shard_map/ppermute | solution.py:35
  59.2 18.1 %copy-start.6 = (bf16[512,64]{0,1:T(8,128)(2,1)S(1)}, bf16[512,64]{0,1:T(8,128)(2,1)}, u32[]{:S(2)}) copy-start(bf16[512,64]{0,1:T(8,128)(2,1)} %copy-done.5) | copy-start | bytes 196612
  59.2 18.1 %copy-start.8 = (bf16[512,64]{0,1:T(8,128)(2,1)S(1)}, bf16[512,64]{0,1:T(8,128)(2,1)}, u32[]{:S(2)}) copy-start(bf16[512,64]{0,1:T(8,128)(2,1)} %copy-done.7) | copy-start | bytes 196612
  77.4 15.3 %copy-start.10 = (bf16[4608,256]{0,1:T(8,128)(2,1)}, bf16[4608,256]{0,1:T(8,128)(2,1)S(1)}, u32[]{:S(2)}) copy-start(bf16[4608,256]{0,1:T(8,128)(2,1)S(1)} %constant_dynamic-update-slice_fusion) | copy-start | bytes 7077892
  126.4 9.8 %collective-permute-start.4 = (bf16[512,512]{0,1:T(8,128)(2,1)S(1)}, bf16[512,512]{0,1:T(8,128)(2,1)S(1)}, u32[]{:S(2)}, u32[]{:S(2)}) collective-permute-start(bf16[512,512]{0,1:T(8,128)(2,1)S(1)} %bitcast.44), channel_id=1, source_target_pairs={{0,1},{1,2},{2,3},{3,4},{4,5},{5,6},{6,7},{7,0},{8,9},{9,10},{10,1... | collective-permute-start | bytes 1572872 | tf_op jit(solution)/shard_map/ppermute | solution.py:18
  136.2 9.8 %collective-permute-start.5 = (bf16[512,512]{0,1:T(8,128)(2,1)S(1)}, bf16[512,512]{0,1:T(8,128)(2,1)S(1)}, u32[]{:S(2)}, u32[]{:S(2)}) collective-permute-start(bf16[512,512]{0,1:T(8,128)(2,1)S(1)} %collective-permute-done.4), channel_id=1, source_target_pairs={{0,1},{1,2},{2,3},{3,4},{4,5},{5,6},{6,7},{7,0},{8,9},{9,10},{10,1... | collective-permute-start | bytes 1572872 | tf_op jit(solution)/shard_map/ppermute | solution.py:18
  136.2 9.8 %collective-permute-start.8 = (bf16[512,512]{0,1:T(8,128)(2,1)S(1)}, bf16[512,512]{0,1:T(8,128)(2,1)S(1)}, u32[]{:S(2)}, u32[]{:S(2)}) collective-permute-start(bf16[512,512]{0,1:T(8,128)(2,1)S(1)} %bitcast.45), channel_id=1, source_target_pairs={{0,7},{1,0},{2,1},{3,2},{4,3},{5,4},{6,5},{7,6},{8,15},{9,8},{10,9... | collective-permute-start | bytes 1572872 | tf_op jit(solution)/shard_map/ppermute | solution.py:21
  146.0 9.8 %collective-permute-start.6 = (bf16[512,512]{0,1:T(8,128)(2,1)S(1)}, bf16[512,512]{0,1:T(8,128)(2,1)S(1)}, u32[]{:S(2)}, u32[]{:S(2)}) collective-permute-start(bf16[512,512]{0,1:T(8,128)(2,1)S(1)} %collective-permute-done.5), channel_id=1, source_target_pairs={{0,1},{1,2},{2,3},{3,4},{4,5},{5,6},{6,7},{7,0},{8,9},{9,10},{10,1... | collective-permute-start | bytes 1572872 | tf_op jit(solution)/shard_map/ppermute | solution.py:18
  146.0 9.8 %collective-permute-start.9 = (bf16[512,512]{0,1:T(8,128)(2,1)S(1)}, bf16[512,512]{0,1:T(8,128)(2,1)S(1)}, u32[]{:S(2)}, u32[]{:S(2)}) collective-permute-start(bf16[512,512]{0,1:T(8,128)(2,1)S(1)} %collective-permute-done.8), channel_id=1, source_target_pairs={{0,7},{1,0},{2,1},{3,2},{4,3},{5,4},{6,5},{7,6},{8,15},{9,8},{10,9... | collective-permute-start | bytes 1572872 | tf_op jit(solution)/shard_map/ppermute | solution.py:21
  155.8 9.9 %collective-permute-start.7 = (bf16[512,512]{0,1:T(8,128)(2,1)S(1)}, bf16[512,512]{0,1:T(8,128)(2,1)}, u32[]{:S(2)}, u32[]{:S(2)}) collective-permute-start(bf16[512,512]{0,1:T(8,128)(2,1)S(1)} %collective-permute-done.6), channel_id=1, source_target_pairs={{0,1},{1,2},{2,3},{3,4},{4,5},{5,6},{6,7},{7,0},{8,9},{9,10},{10,1... | collective-permute-start | bytes 1572872 | tf_op jit(solution)/shard_map/ppermute | solution.py:18
  155.8 12.7 %copy-start.11 = (bf16[4096,512]{1,0:T(8,128)(2,1)S(1)}, bf16[4096,512]{1,0:T(8,128)(2,1)}, u32[]{:S(2)}) copy-start(bf16[4096,512]{1,0:T(8,128)(2,1)} %param.12) | copy-start | bytes 12582916
  155.8 11.3 %collective-permute-start.10 = (bf16[512,512]{0,1:T(8,128)(2,1)S(1)}, bf16[512,512]{0,1:T(8,128)(2,1)S(1)}, u32[]{:S(2)}, u32[]{:S(2)}) collective-permute-start(bf16[512,512]{0,1:T(8,128)(2,1)S(1)} %collective-permute-done.9), channel_id=1, source_target_pairs={{0,7},{1,0},{2,1},{3,2},{4,3},{5,4},{6,5},{7,6},{8,15},{9,8},{10,9... | collective-permute-start | bytes 1572872 | tf_op jit(solution)/shard_map/ppermute | solution.py:21
  168.5 3.3 %copy-start.1 = (bf16[4096,128]{1,0:T(8,128)(2,1)S(1)}, bf16[4096,128]{1,0:T(8,128)(2,1)}, u32[]{:S(2)}) copy-start(bf16[4096,128]{1,0:T(8,128)(2,1)} %param.11) | copy-start | bytes 3145732
